TPU v7x, 1024 devices: a whole 4x4x32 slice. The times are simulated.
1024 devices in a mesh: gx: 8 (over x, core), gy: 16 (over z_lo), gz: 8 (over y, z_hi).
Axes of the slice: x: 4, y: 4, z: 32 (z_hi: 2, z_lo: 16; z = z_hi * 16 + z_lo), core: 2. Of those that a mesh axis runs over, the one named last changes fastest.
Arguments:
- schur: bfloat16 [8, 16, 8, 1024, 1024], P('gx', 'gy', 'gz'), may hold values from -10 to 10, as said below
- rhs_local: float32 [8, 16, 8, 32, 1024], P('gx', 'gy', 'gz'), may hold values from -40 to 40
- block_map: int32 [8, 16, 8, 8], P('gx', 'gy', 'gz'), may hold values from 0 to 7, each once within a row
Outputs:
- solution: float32 [8, 16, 8, 32, 1024], P('gx', 'gy', 'gz')
- residual: float32 [8, 16, 8, 32, 1024], P('gx', 'gy', 'gz')
Inputs may be any that keep to these rules, and one draw needn't show every extreme that they name: `schur`: each local Schur complement is symmetric positive definite.
All inputs are finite; a program needn't handle non-finite values.
Results may differ from a plain program's by a relative error of at most 0.0003.
Values sent between devices are 32-bit elements; how exact they have to be, the bound alone decides.
No kernel may reach another device: no remote copies, remote signals or barrier semaphores. Data moves between devices by JAX's collectives and lax.ppermute only.
A program may use at most 64 MiB of HBM per device.

v0:
```python
import jax
import jax.numpy as jnp
from jax import lax
from jax.experimental import pallas as pl
from jax.experimental.pallas import tpu as pltpu
from jax.sharding import PartitionSpec as P


B = 128
M = 1024
R = 32
F32 = jnp.float32
HIGHEST = lax.Precision.HIGHEST
ORDER = (6, 7, 0, 1, 2, 3, 4, 5)
PANEL = 2 * B
GROUPS = 4
VMEM = pl.BlockSpec(memory_space=pltpu.VMEM)
SMEM = pl.BlockSpec(memory_space=pltpu.SMEM)


def mm(a, b, dims=((1,), (0,))):
    return lax.dot_general(
        a, b, (dims, ((), ())), precision=HIGHEST, preferred_element_type=F32
    )


def mmt(a, b):
    return mm(a, b, ((1,), (1,)))


def block(pos):
    return pl.ds(pl.multiple_of(pos * B, B), B)


def spread(row):
    return jnp.broadcast_to(row, (8, B))


def pivot_group(rows, g, lane, sub):
    base = 8 * g
    inside = (lane >= base) & (lane < base + 8)
    mine = [
        jnp.take_along_axis(rows[g], jnp.full((8, B), base + j, jnp.int32), axis=1)
        for j in range(8)
    ]
    own = jnp.where(inside, jnp.where(lane - base == sub, 1.0, 0.0), rows[g])
    for p in range(0, 8, 2):
        c0, c1 = mine[p], mine[p + 1]
        a, b, c = spread(c0[p : p + 1]), spread(c1[p : p + 1]), spread(c1[p + 1 : p + 2])
        scale = 1.0 / (a * c - b * b)
        i00, i01, i11 = c * scale, -b * scale, a * scale
        first, second = sub == p, sub == p + 1

        def clear(x):
            x0, x1 = spread(x[p : p + 1]), spread(x[p + 1 : p + 2])
            n0, n1 = i00 * x0 + i01 * x1, i01 * x0 + i11 * x1
            return jnp.where(first, n0, jnp.where(second, n1, x - c0 * n0 - c1 * n1))

        for j in range(p + 2, 8):
            mine[j] = clear(mine[j])
        own = clear(own)
    parts = [spread(own[j : j + 1]) for j in range(8)]
    new = []
    for v, old in enumerate(rows):
        out = own
        if v != g:
            out = jnp.where(inside, 0.0, old)
            for j in range(8):
                out = out - spread(old[:, base + j : base + j + 1]) * parts[j]
        new.append(out)
    return new


def inverse(rows):
    lane = lax.broadcasted_iota(jnp.int32, (8, B), 1)
    sub = lax.broadcasted_iota(jnp.int32, (8, B), 0)

    def body(_, carry):
        rows = list(carry)
        for g in range(GROUPS):
            rows = pivot_group(rows, g, lane, sub)
        rows = rows[GROUPS:] + rows[:GROUPS]
        return tuple(pltpu.roll(row, B - 8 * GROUPS, 1) for row in rows)

    return lax.fori_loop(0, 16 // GROUPS, body, tuple(rows))


def inverse_of(ref, row, col, out):
    rows = [ref[row + 8 * v : row + 8 * v + 8, col : col + B] for v in range(16)]
    for v, value in enumerate(inverse(rows)):
        out[8 * v : 8 * v + 8, :] = value


def eliminate(panel, kept, inv):
    inverse_of(panel, 0, 0, inv)
    below = panel[B:, :B]
    scaled = mm(below, inv[...])
    kept[B : panel.shape[0], :B] = below
    panel[B:, :B] = scaled
    panel[B:, B:] -= mmt(scaled, below[:B])
    inverse_of(panel, B, B, inv)
    below = panel[PANEL:, B:]
    kept[PANEL : panel.shape[0], B:] = below
    panel[PANEL:, B:] = mm(below, inv[...])


def update(panel, kept, later, gap):
    later[...] -= mmt(panel[PANEL * gap :, :], kept[PANEL * gap : PANEL * (gap + 1), :])


def pack_kernel(map_ref, schur_ref, rhs_ref, *sends):
    for face in range(6):
        at = block(map_ref[face])
        sends[face][:B, :] = schur_ref[at, at].astype(F32)
        sends[face][B:, :] = rhs_ref[:, at]


def first_kernel(map_ref, schur_ref, rhs_ref, c0, c1, c2, c3, kept, inv):
    panels = (c0, c1, c2, c3)
    for j in range(8):
        panel, left = panels[j // 2], (j % 2) * B
        col = block(map_ref[ORDER[j]])
        for i in range(j // 2 * 2, 8):
            top = (i - j // 2 * 2) * B
            panel[top : top + B, left : left + B] = schur_ref[
                block(map_ref[ORDER[i]]), col
            ].astype(F32)
        panel[panel.shape[0] - R :, left : left + B] = rhs_ref[:, col]
    eliminate(c0, kept, inv)
    for gap in (1, 2, 3):
        update(c0, kept, panels[gap], gap)


def add_received(panel, half, received):
    rows = slice(half * B, half * B + B)
    panel[rows, rows] += received[:B, :]
    panel[panel.shape[0] - R :, rows] += received[B:, :]


def middle_kernel(i1, i2, i3, x0, x1, y0, y1, c1, c2, c3, kept, inv):
    c1[...], c2[...], c3[...] = i1[...], i2[...], i3[...]
    for panel, pair in ((c1, (x0, x1)), (c2, (y0, y1))):
        for half in range(2):
            add_received(panel, half, pair[half])
    eliminate(c1, kept, inv)
    update(c1, kept, c2, 1)
    update(c1, kept, c3, 2)
    eliminate(c2, kept, inv)
    update(c2, kept, c3, 1)


def solve_back(panel, later):
    height = panel.shape[0] - R
    acc = panel[height:, :]
    if later is not None:
        acc = acc - mm(later, panel[PANEL:height, :])
    high = acc[:, B:]
    return acc[:, :B] - mm(high, panel[B:PANEL, :B]), high


def last_kernel(i3, z0, z1, low, high, c3, kept, inv):
    c3[...] = i3[...]
    add_received(c3, 0, z0)
    add_received(c3, 1, z1)
    eliminate(c3, kept, inv)
    low[...], high[...] = solve_back(c3, None)


def back_kernel(c0, c1, c2, z0, z1, zeta, *sends):
    zeta[:, 6 * B : 7 * B] = z0[...]
    zeta[:, 7 * B :] = z1[...]
    for step in (2, 1, 0):
        low, high = solve_back((c0, c1, c2)[step], zeta[:, PANEL * (step + 1) :])
        zeta[:, PANEL * step : PANEL * step + B] = low
        zeta[:, PANEL * step + B : PANEL * (step + 1)] = high
    for face in range(4):
        sends[face][...] = zeta[:, (face + 2) * B : (face + 3) * B]


def apply_kernel(map_ref, schur_ref, rhs_ref, zeta_ref, *rest):
    received, sent = rest[:6], rest[6:12]
    zeta, image, residual, gram = rest[12:16]
    sends, parts = rest[16:22], rest[22]
    rho = jnp.zeros((R, R), F32)
    for q in range(8):
        at = block(map_ref[ORDER[q]])
        local = zeta_ref[:, q * B : (q + 1) * B]
        right = rhs_ref[:, at]
        whole = local
        if q >= 2:
            right = right + sent[q - 2][B:, :]
            whole = local + received[q - 2][...]
        residual[:, at] = right
        zeta[:, at] = whole
        rho = rho + mmt(local, right)
        high = whole.astype(jnp.bfloat16)
        left = whole - high.astype(F32)
        middle = left.astype(jnp.bfloat16)
        parts[:R, at] = high
        parts[R : 2 * R, at] = middle
        parts[2 * R :, at] = (left - middle.astype(F32)).astype(jnp.bfloat16)
    full = jnp.dot(parts[...], schur_ref[...], preferred_element_type=F32)
    image[...] = full[2 * R :] + full[R : 2 * R] + full[:R]
    gram[:R, :] = rho
    gram[R:, :] = mmt(zeta[...], image[...])
    for face in range(6):
        sends[face][...] = image[:, block(map_ref[face])]


def finish_kernel(map_ref, gram_ref, zeta_ref, image_ref, residual_ref, *rest):
    received, (solution_ref, out_ref, image) = rest[:6], rest[6:]
    sub = lax.broadcasted_iota(jnp.int32, (8, 2 * R), 0)
    joined = jnp.concatenate([gram_ref[:R, :], gram_ref[R:, :]], axis=1)
    rows = [joined[8 * v : 8 * v + 8, :] for v in range(R // 8)]
    for p in range(R):
        group, s = divmod(p, 8)
        pivot = rows[group][s : s + 1, :]
        pivot = pivot / pivot[:, R + p : R + p + 1]
        new = []
        for v, old in enumerate(rows):
            out = old - old[:, R + p : R + p + 1] * pivot
            new.append(jnp.where(sub == s, pivot, out) if v == group else out)
        rows = new
    alpha = jnp.concatenate(rows, axis=0)[:, :R]
    image[...] = image_ref[...]
    for face in range(6):
        image[:, block(map_ref[face])] += received[face][...]
    solution_ref[...] = mm(alpha, zeta_ref[...], ((0,), (0,)))
    out_ref[...] = residual_ref[...] - mm(alpha, image[...], ((0,), (0,)))


def arr(*shape):
    return jax.ShapeDtypeStruct(shape, F32)


def call(kernel, outs, args, scratch=(), flops=0):
    in_specs = [SMEM if a.dtype == jnp.int32 else VMEM for a in args]
    moved = sum(a.size * a.dtype.itemsize for a in args) + sum(4 * o.size for o in outs)
    return pl.pallas_call(
        kernel,
        out_shape=outs,
        in_specs=in_specs,
        out_specs=[VMEM] * len(outs),
        scratch_shapes=scratch,
        cost_estimate=pl.CostEstimate(flops=flops, bytes_accessed=moved, transcendentals=0),
    )(*args)


def exchange(axis, low, high):
    up = [(i, i + 1) for i in range(lax.axis_size(axis) - 1)]
    down = [(j, i) for i, j in up]
    before = lax.ppermute(high, axis, up)
    after = lax.ppermute(low, axis, down)
    return before, after


def exchange_all(sends):
    along_z = exchange("gz", *sends[4:])
    return *exchange("gx", *sends[:2]), *exchange("gy", *sends[2:4]), *along_z


def total(gram):
    nx, ny, nz = (lax.axis_size(axis) for axis in ("gx", "gy", "gz"))
    layer = [[x * nz + y + h for x in range(nx) for y in range(0, nz, 2)] for h in range(2)]
    column = [[y * nz + k + h for y in range(ny) for h in range(2)] for k in range(0, nz, 2)]

    def swap(x, axes, groups):
        return lax.all_to_all(x, axes, 0, 0, axis_index_groups=groups, tiled=True)

    pieces, depth = len(layer[0]), len(column[0])
    part = swap(gram.reshape(pieces, -1), ("gx", "gz"), layer).sum(0)
    part = swap(jnp.broadcast_to(part, (depth, part.size)), ("gy", "gz"), column).sum(0)
    whole = swap(jnp.broadcast_to(part, (pieces, part.size)), ("gx", "gz"), layer)
    return whole.reshape(gram.shape)


def step(schur, rhs_local, block_map):
    stored = schur[0, 0, 0]
    place = block_map[0, 0, 0]
    right_side = rhs_local[0, 0, 0]
    heights = [M - PANEL * s + R for s in range(4)]
    panels = [arr(h, PANEL) for h in heights]
    inv = pltpu.VMEM((B, B), F32)

    def work(s):
        return [pltpu.VMEM((heights[s], PANEL), F32), inv]

    sends = call(pack_kernel, [arr(B + R, B)] * 6, (place, stored, right_side))
    met = exchange_all(sends)
    c0, c1, c2, c3 = call(first_kernel, panels, (place, stored, right_side), work(0), 10**10)
    c1, c2, c3 = call(middle_kernel, panels[1:], (c1, c2, c3, *met[:4]), work(1), 2 * 10**10)
    z_faces = call(
        last_kernel,
        [arr(R, B)] * 2,
        (c3, *met[4:]),
        [pltpu.VMEM((heights[3], PANEL), F32)] + work(3),
        10**10,
    )
    z_met = exchange("gz", *z_faces)
    zeta_local, *faces = call(
        back_kernel, [arr(R, M)] + [arr(R, B)] * 4, (c0, c1, c2, *z_faces), (), 10**9
    )
    zeta_met = (*exchange("gx", *faces[:2]), *exchange("gy", *faces[2:]), *z_met)
    zeta, image, residual, gram, *faces = call(
        apply_kernel,
        [arr(R, M)] * 3 + [arr(2 * R, R)] + [arr(R, B)] * 6,
        (place, stored, right_side, zeta_local, *zeta_met, *met),
        [pltpu.VMEM((3 * R, M), jnp.bfloat16)],
        10**9,
    )
    image_met = exchange_all(faces)
    gram = total(gram)
    solution, residual = call(
        finish_kernel,
        [arr(R, M)] * 2,
        (place, gram, zeta, image, residual, *image_met),
        [pltpu.VMEM((R, M), F32)],
        10**9,
    )
    return (solution[None, None, None], residual[None, None, None])


def solution(mesh):
    in_specs = (
        P("gx", "gy", "gz", None, None),
        P("gx", "gy", "gz", None, None),
        P("gx", "gy", "gz", None),
    )
    out_specs = (P("gx", "gy", "gz", None, None), P("gx", "gy", "gz", None, None))
    return jax.shard_map(step, mesh=mesh, in_specs=in_specs, out_specs=out_specs, check_vma=False)
```

profile of v0, /device:TPU:34, one launch (start us, length us, event | category | flops | bytes accessed | tf_op | source)
XLA Modules:
  0.0 251.1 jit_solution(911410395641817863)
XLA Ops:
  0.6 2.4 shard_map.51
  3.1 1.9 collective-permute-start
  5.0 3.6 %collective-permute-start.1 = (f32[160,128]{1,0:T(8,128)}, f32[160,128]{1,0:T(8,128)S(1)}, u32[]{:S(2)}, u32[]{:S(2)}) collective-permute-start(f32[160,128]{1,0:T(8,128)} %get-tuple-element.39), channel_id=1, source_target_pairs={{128,0},{256,128},{384,256},{512,384},{640,512},{768,640},{896,768... | collective-permute-start | bytes 245768 | tf_op jit(solution)/shard_map/ppermute | solution.py:253
  8.6 3.8 %collective-permute-start.2 = (f32[160,128]{1,0:T(8,128)}, f32[160,128]{1,0:T(8,128)S(1)}, u32[]{:S(2)}, u32[]{:S(2)}) collective-permute-start(f32[160,128]{1,0:T(8,128)} %get-tuple-element.40), channel_id=1, source_target_pairs={{0,8},{8,16},{16,24},{24,32},{32,40},{40,48},{48,56},{56,64},{64,7... | collective-permute-start | bytes 245768 | tf_op jit(solution)/shard_map/ppermute | solution.py:252
  12.5 2.0 collective-permute-start.3
  14.5 28.2 %collective-permute-start.4 = (f32[160,128]{1,0:T(8,128)}, f32[160,128]{1,0:T(8,128)S(1)}, u32[]{:S(2)}, u32[]{:S(2)}) collective-permute-start(f32[160,128]{1,0:T(8,128)} %get-tuple-element.45), channel_id=1, source_target_pairs={{0,1},{1,2},{2,3},{3,4},{4,5},{5,6},{6,7},{8,9},{9,10},{10,11},{11... | collective-permute-start | bytes 245768 | tf_op jit(solution)/shard_map/ppermute | solution.py:252
  42.7 15.0 %shard_map.50 = (f32[1056,256]{1,0:T(8,128)}, f32[800,256]{1,0:T(8,128)}, f32[544,256]{1,0:T(8,128)}, f32[288,256]{1,0:T(8,128)}) custom-call(s32[8]{0:T(128)} %bitcast.16, bf16[1024,1024]{1,0:T(8,128)(2,1)} %bitcast.8, f32[32,1024]{1,0:T(8,128)} %bitcast.11), custom_call_target="tpu_custom_call" | custom-call | flops 10000000000 | bytes 4980768 | tf_op jit(solution)/shard_map/pallas_call | solution.py:239
  57.7 1.5 collective-permute-start.5
  59.9 23.2 %shard_map.52 = (f32[800,256]{1,0:T(8,128)}, f32[544,256]{1,0:T(8,128)}, f32[288,256]{1,0:T(8,128)}) custom-call(f32[800,256]{1,0:T(8,128)} %get-tuple-element.35.i1, f32[544,256]{1,0:T(8,128)} %get-tuple-element.36.i2, f32[288,256]{1,0:T(8,128)} %get-tuple-element.37.i3, f32[160,128]{1,0:T(8,128)} %copy-done, f32[160,128]{1,0:T(8,128)} %copy-done.1, ...), custom_call_target="tpu_custom_call" | custom-call | flops 20000000000 | bytes 3670016 | tf_op jit(solution)/shard_map/pallas_call | solution.py:239
  83.1 10.6 %collective-permute-done.5.z1.rest_11_ = f32[160,128]{1,0:T(8,128)S(1)} collective-permute-done((f32[160,128]{1,0:T(8,128)S(1)}, f32[160,128]{1,0:T(8,128)S(1)}, u32[]{:S(2)}, u32[]{:S(2)}) %collective-permute-start.5) | collective-permute-done | bytes 81952 | tf_op jit(solution)/shard_map/ppermute | solution.py:253
  94.3 10.8 %shard_map.53 = (f32[32,128]{1,0:T(8,128)}, f32[32,128]{1,0:T(8,128)}) custom-call(f32[288,256]{1,0:T(8,128)} %get-tuple-element.44.i3, f32[160,128]{1,0:T(8,128)} %copy-done.4, f32[160,128]{1,0:T(8,128)} %copy-done.5), custom_call_target="tpu_custom_call" | custom-call | flops 10000000000 | bytes 491520 | tf_op jit(solution)/shard_map/pallas_call | solution.py:239
  105.1 4.4 %shard_map.54 = (f32[32,1024]{1,0:T(8,128)}, f32[32,128]{1,0:T(8,128)}, f32[32,128]{1,0:T(8,128)}, f32[32,128]{1,0:T(8,128)}, f32[32,128]{1,0:T(8,128)}) custom-call(f32[1056,256]{1,0:T(8,128)} %get-tuple-element.34.c0, f32[800,256]{1,0:T(8,128)} %get-tuple-element.42.c1, f32[544,256]{1,0:T(8,128)} %get-tuple-element.43.c2, f32[32,128]{1,0:T(8,128)} %get-tuple-element.47.z0, ...), custom_call_target="tpu_custom_call" | custom-call | flops 1000000000 | bytes 2686976 | tf_op jit(solution)/shard_map/pallas_call | solution.py:239
  109.5 1.9 collective-permute-start.6
  111.4 12.3 %collective-permute-start.10 = (f32[32,128]{1,0:T(8,128)S(1)}, f32[32,128]{1,0:T(8,128)S(1)}, u32[]{:S(2)}, u32[]{:S(2)}) collective-permute-start(f32[32,128]{1,0:T(8,128)S(1)} %copy-done.16), channel_id=1, source_target_pairs={{0,1},{1,2},{2,3},{3,4},{4,5},{5,6},{6,7},{8,9},{9,10},{10,11},{11... | collective-permute-start | bytes 49160 | tf_op jit(solution)/shard_map/ppermute | solution.py:252
  123.8 3.4 %collective-permute-start.7 = (f32[32,128]{1,0:T(8,128)}, f32[32,128]{1,0:T(8,128)S(1)}, u32[]{:S(2)}, u32[]{:S(2)}) collective-permute-start(f32[32,128]{1,0:T(8,128)} %get-tuple-element.51), channel_id=1, source_target_pairs={{128,0},{256,128},{384,256},{512,384},{640,512},{768,640},{896,768... | collective-permute-start | bytes 49160 | tf_op jit(solution)/shard_map/ppermute | solution.py:253
  127.1 2.9 %collective-permute-start.8 = (f32[32,128]{1,0:T(8,128)}, f32[32,128]{1,0:T(8,128)S(1)}, u32[]{:S(2)}, u32[]{:S(2)}) collective-permute-start(f32[32,128]{1,0:T(8,128)} %get-tuple-element.52), channel_id=1, source_target_pairs={{0,8},{8,16},{16,24},{24,32},{32,40},{40,48},{48,56},{56,64},{64,7... | collective-permute-start | bytes 49160 | tf_op jit(solution)/shard_map/ppermute | solution.py:252
  130.1 2.9 %collective-permute-start.9 = (f32[32,128]{1,0:T(8,128)}, f32[32,128]{1,0:T(8,128)S(1)}, u32[]{:S(2)}, u32[]{:S(2)}) collective-permute-start(f32[32,128]{1,0:T(8,128)} %get-tuple-element.53), channel_id=1, source_target_pairs={{8,0},{16,8},{24,16},{32,24},{40,32},{48,40},{56,48},{64,56},{72,6... | collective-permute-start | bytes 49160 | tf_op jit(solution)/shard_map/ppermute | solution.py:253
  133.0 1.3 collective-permute-start.11
  134.4 1.6 collective-permute-done.9.rest_3_
  135.9 21.1 %collective-permute-done.11.rest_5_ = f32[32,128]{1,0:T(8,128)S(1)} collective-permute-done((f32[32,128]{1,0:T(8,128)S(1)}, f32[32,128]{1,0:T(8,128)S(1)}, u32[]{:S(2)}, u32[]{:S(2)}) %collective-permute-start.11) | collective-permute-done | bytes 16416 | tf_op jit(solution)/shard_map/ppermute | solution.py:253
  157.6 3.4 %shard_map.55 = (f32[32,1024]{1,0:T(8,128)}, f32[32,1024]{1,0:T(8,128)}, f32[32,1024]{1,0:T(8,128)}, f32[64,32]{1,0:T(8,128)}, f32[32,128]{1,0:T(8,128)}, /*inde...) custom-call(s32[8]{0:T(128)} %bitcast.17, ...), custom_call_target="tpu_custom_call" | custom-call | flops 1000000000 | bytes 3448864 | tf_op jit(solution)/shard_map/pallas_call | solution.py:239
  161.9 13.6 %all_to_all.21 = f32[32,1,64]{2,1,0:T(1,128)S(1)} all-to-all(f32[32,1,64]{2,1,0:T(1,128)S(1)} %bitcast.13), channel_id=1, replica_groups={{0,2,4,6,128,130,132,134,256,258,260,262,384,386,388,390,512,514,516,51..., dimensions={0} | all-to-all | bytes 16384 | tf_op jit(solution)/shard_map/all_to_all | solution.py:268
  176.1 11.8 %all-to-all-start.1 = ((f32[32,1,64]{2,1,0:T(1,128)}), f32[32,1,64]{2,1,0:T(1,128)S(1)}, u32[]{:S(2)}, u32[]{:S(2)}) async-start(f32[32,1,64]{2,1,0:T(1,128)} %broadcast_in_dim.12), calls=%async_computation.1 | async-start | bytes 32768 | tf_op jit(solution)/shard_map/all_to_all | solution.py:268
  187.9 1.9 collective-permute-start.12
  189.8 3.6 %collective-permute-start.13 = (f32[32,128]{1,0:T(8,128)}, f32[32,128]{1,0:T(8,128)S(1)}, u32[]{:S(2)}, u32[]{:S(2)}) collective-permute-start(f32[32,128]{1,0:T(8,128)} %get-tuple-element.59), channel_id=1, source_target_pairs={{128,0},{256,128},{384,256},{512,384},{640,512},{768,640},{896,768... | collective-permute-start | bytes 49160 | tf_op jit(solution)/shard_map/ppermute | solution.py:253
  193.5 3.4 %collective-permute-start.14 = (f32[32,128]{1,0:T(8,128)}, f32[32,128]{1,0:T(8,128)S(1)}, u32[]{:S(2)}, u32[]{:S(2)}) collective-permute-start(f32[32,128]{1,0:T(8,128)} %get-tuple-element.60), channel_id=1, source_target_pairs={{0,8},{8,16},{16,24},{24,32},{32,40},{40,48},{48,56},{56,64},{64,7... | collective-permute-start | bytes 49160 | tf_op jit(solution)/shard_map/ppermute | solution.py:252
  196.9 2.5 collective-permute-start.15
  199.4 20.8 %collective-permute-start.16 = (f32[32,128]{1,0:T(8,128)}, f32[32,128]{1,0:T(8,128)S(1)}, u32[]{:S(2)}, u32[]{:S(2)}) collective-permute-start(f32[32,128]{1,0:T(8,128)} %get-tuple-element.62), channel_id=1, source_target_pairs={{0,1},{1,2},{2,3},{3,4},{4,5},{5,6},{6,7},{8,9},{9,10},{10,11},{11... | collective-permute-start | bytes 49160 | tf_op jit(solution)/shard_map/ppermute | solution.py:252
  220.2 1.3 collective-permute-start.17
  221.5 13.7 %all_to_all.22 = f32[32,1,64]{2,1,0:T(1,128)S(1)} all-to-all(f32[32,1,64]{2,1,0:T(1,128)S(1)} %broadcast_in_dim.13), channel_id=1, replica_groups={{0,2,4,6,128,130,132,134,256,258,260,262,384,386,388,390,512,514,516,51..., dimensions={0} | all-to-all | bytes 16384 | tf_op jit(solution)/shard_map/all_to_all | solution.py:268
  237.1 8.4 %collective-permute-done.17.rest_5_ = f32[32,128]{1,0:T(8,128)S(1)} collective-permute-done((f32[32,128]{1,0:T(8,128)}, f32[32,128]{1,0:T(8,128)S(1)}, u32[]{:S(2)}, u32[]{:S(2)}) %collective-permute-start.17) | collective-permute-done | bytes 16416 | tf_op jit(solution)/shard_map/ppermute | solution.py:253
  246.2 4.9 %shard_map.56 = (f32[32,1024]{1,0:T(8,128)}, f32[32,1024]{1,0:T(8,128)}) custom-call(s32[8]{0:T(128)} %bitcast.18, f32[64,32]{1,0:T(8,128)} %reshape.20.gram_ref, f32[32,1024]{1,0:T(8,128)} %get-tuple-element.55.zeta_ref, f32[32,1024]{1,0:T(8,128)} %get-tuple-element.56.image_ref, f32[32,1024]{1,0:T(8,128)} %get-tuple-element.57.residual_ref, ...), custom_call_target="tpu_custom_call" | custom-call | flops 1000000000 | bytes 761888 | tf_op jit(solution)/shard_map/pallas_call | solution.py:239
  (65 shorter events, 5.9 us)
Async XLA Ops:
  3.1 54.7 %collective-permute-start = (f32[160,128]{1,0:T(8,128)}, f32[160,128]{1,0:T(8,128)S(1)}, u32[]{:S(2)}, u32[]{:S(2)}) collective-permute-start(f32[160,128]{1,0:T(8,128)} %get-tuple-element.38), channel_id=1, source_target_pairs={{0,128},{128,256},{256,384},{384,512},{512,640},{640,768},{768,896... | collective-permute-start | bytes 245768 | tf_op jit(solution)/shard_map/ppermute | solution.py:252
  5.0 54.2 %collective-permute-start.1 = (f32[160,128]{1,0:T(8,128)}, f32[160,128]{1,0:T(8,128)S(1)}, u32[]{:S(2)}, u32[]{:S(2)}) collective-permute-start(f32[160,128]{1,0:T(8,128)} %get-tuple-element.39), channel_id=1, source_target_pairs={{128,0},{256,128},{384,256},{512,384},{640,512},{768,640},{896,768... | collective-permute-start | bytes 245768 | tf_op jit(solution)/shard_map/ppermute | solution.py:253
  8.6 50.6 %collective-permute-start.2 = (f32[160,128]{1,0:T(8,128)}, f32[160,128]{1,0:T(8,128)S(1)}, u32[]{:S(2)}, u32[]{:S(2)}) collective-permute-start(f32[160,128]{1,0:T(8,128)} %get-tuple-element.40), channel_id=1, source_target_pairs={{0,8},{8,16},{16,24},{24,32},{32,40},{40,48},{48,56},{56,64},{64,7... | collective-permute-start | bytes 245768 | tf_op jit(solution)/shard_map/ppermute | solution.py:252
  12.5 46.8 %collective-permute-start.3 = (f32[160,128]{1,0:T(8,128)}, f32[160,128]{1,0:T(8,128)S(1)}, u32[]{:S(2)}, u32[]{:S(2)}) collective-permute-start(f32[160,128]{1,0:T(8,128)} %get-tuple-element.41), channel_id=1, source_target_pairs={{8,0},{16,8},{24,16},{32,24},{40,32},{48,40},{56,48},{64,56},{72,6... | collective-permute-start | bytes 245768 | tf_op jit(solution)/shard_map/ppermute | solution.py:253
  14.5 43.2 %copy-start.6 = (f32[160,128]{1,0:T(8,128)S(1)}, f32[160,128]{1,0:T(8,128)}, u32[]{:S(2)}) copy-start(f32[160,128]{1,0:T(8,128)} %get-tuple-element.46) | copy-start | bytes 245764
  14.5 68.6 %collective-permute-start.4 = (f32[160,128]{1,0:T(8,128)}, f32[160,128]{1,0:T(8,128)S(1)}, u32[]{:S(2)}, u32[]{:S(2)}) collective-permute-start(f32[160,128]{1,0:T(8,128)} %get-tuple-element.45), channel_id=1, source_target_pairs={{0,1},{1,2},{2,3},{3,4},{4,5},{5,6},{6,7},{8,9},{9,10},{10,11},{11... | collective-permute-start | bytes 245768 | tf_op jit(solution)/shard_map/ppermute | solution.py:252
  57.7 36.0 %collective-permute-start.5 = (f32[160,128]{1,0:T(8,128)S(1)}, f32[160,128]{1,0:T(8,128)S(1)}, u32[]{:S(2)}, u32[]{:S(2)}) collective-permute-start(f32[160,128]{1,0:T(8,128)S(1)} %copy-done.6), channel_id=1, source_target_pairs={{1,0},{2,1},{3,2},{4,3},{5,4},{6,5},{7,6},{9,8},{10,9},{11,10},{12... | collective-permute-start | bytes 245768 | tf_op jit(solution)/shard_map/ppermute | solution.py:253
  83.1 10.6 %copy-start.4 = (f32[160,128]{1,0:T(8,128)}, f32[160,128]{1,0:T(8,128)S(1)}, u32[]{:S(2)}) copy-start(f32[160,128]{1,0:T(8,128)S(1)} %collective-permute-done.4.z0.rest_10_) | copy-start | bytes 245764
  105.1 27.9 %copy-start.14 = (f32[32,128]{1,0:T(8,128)S(1)}, f32[32,128]{1,0:T(8,128)}, u32[]{:S(2)}) copy-start(f32[32,128]{1,0:T(8,128)} %get-tuple-element.47.z0) | copy-start | bytes 49156
  109.5 23.5 %collective-permute-start.6 = (f32[32,128]{1,0:T(8,128)}, f32[32,128]{1,0:T(8,128)S(1)}, u32[]{:S(2)}, u32[]{:S(2)}) collective-permute-start(f32[32,128]{1,0:T(8,128)} %get-tuple-element.50), channel_id=1, source_target_pairs={{0,128},{128,256},{256,384},{384,512},{512,640},{640,768},{768,896... | collective-permute-start | bytes 49160 | tf_op jit(solution)/shard_map/ppermute | solution.py:252
  111.4 24.5 %collective-permute-start.10 = (f32[32,128]{1,0:T(8,128)S(1)}, f32[32,128]{1,0:T(8,128)S(1)}, u32[]{:S(2)}, u32[]{:S(2)}) collective-permute-start(f32[32,128]{1,0:T(8,128)S(1)} %copy-done.16), channel_id=1, source_target_pairs={{0,1},{1,2},{2,3},{3,4},{4,5},{5,6},{6,7},{8,9},{9,10},{10,11},{11... | collective-permute-start | bytes 49160 | tf_op jit(solution)/shard_map/ppermute | solution.py:252
  123.8 10.6 %collective-permute-start.7 = (f32[32,128]{1,0:T(8,128)}, f32[32,128]{1,0:T(8,128)S(1)}, u32[]{:S(2)}, u32[]{:S(2)}) collective-permute-start(f32[32,128]{1,0:T(8,128)} %get-tuple-element.51), channel_id=1, source_target_pairs={{128,0},{256,128},{384,256},{512,384},{640,512},{768,640},{896,768... | collective-permute-start | bytes 49160 | tf_op jit(solution)/shard_map/ppermute | solution.py:253
  127.1 7.2 %collective-permute-start.8 = (f32[32,128]{1,0:T(8,128)}, f32[32,128]{1,0:T(8,128)S(1)}, u32[]{:S(2)}, u32[]{:S(2)}) collective-permute-start(f32[32,128]{1,0:T(8,128)} %get-tuple-element.52), channel_id=1, source_target_pairs={{0,8},{8,16},{16,24},{24,32},{32,40},{40,48},{48,56},{56,64},{64,7... | collective-permute-start | bytes 49160 | tf_op jit(solution)/shard_map/ppermute | solution.py:252
  130.1 5.8 %collective-permute-start.9 = (f32[32,128]{1,0:T(8,128)}, f32[32,128]{1,0:T(8,128)S(1)}, u32[]{:S(2)}, u32[]{:S(2)}) collective-permute-start(f32[32,128]{1,0:T(8,128)} %get-tuple-element.53), channel_id=1, source_target_pairs={{8,0},{16,8},{24,16},{32,24},{40,32},{48,40},{56,48},{64,56},{72,6... | collective-permute-start | bytes 49160 | tf_op jit(solution)/shard_map/ppermute | solution.py:253
  133.0 24.0 %copy-start.10 = (f32[32,128]{1,0:T(8,128)}, f32[32,128]{1,0:T(8,128)S(1)}, u32[]{:S(2)}) copy-start(f32[32,128]{1,0:T(8,128)S(1)} %collective-permute-done.6.rest_0_) | copy-start | bytes 49156
  133.0 24.0 %collective-permute-start.11 = (f32[32,128]{1,0:T(8,128)S(1)}, f32[32,128]{1,0:T(8,128)S(1)}, u32[]{:S(2)}, u32[]{:S(2)}) collective-permute-start(f32[32,128]{1,0:T(8,128)S(1)} %copy-done.14), channel_id=1, source_target_pairs={{1,0},{2,1},{3,2},{4,3},{5,4},{6,5},{7,6},{9,8},{10,9},{11,10},{12... | collective-permute-start | bytes 49160 | tf_op jit(solution)/shard_map/ppermute | solution.py:253
  134.3 22.7 %copy-start.15 = (f32[32,128]{1,0:T(8,128)}, f32[32,128]{1,0:T(8,128)S(1)}, u32[]{:S(2)}) copy-start(f32[32,128]{1,0:T(8,128)S(1)} %collective-permute-done.7.rest_1_) | copy-start | bytes 49156
  134.3 22.6 %copy-start.17 = (f32[32,128]{1,0:T(8,128)}, f32[32,128]{1,0:T(8,128)S(1)}, u32[]{:S(2)}) copy-start(f32[32,128]{1,0:T(8,128)S(1)} %collective-permute-done.8.rest_2_) | copy-start | bytes 49156
  135.9 21.1 %copy-start.18 = (f32[32,128]{1,0:T(8,128)}, f32[32,128]{1,0:T(8,128)S(1)}, u32[]{:S(2)}) copy-start(f32[32,128]{1,0:T(8,128)S(1)} %collective-permute-done.9.rest_3_) | copy-start | bytes 49156
  135.9 21.1 %copy-start.12 = (f32[32,128]{1,0:T(8,128)}, f32[32,128]{1,0:T(8,128)S(1)}, u32[]{:S(2)}) copy-start(f32[32,128]{1,0:T(8,128)S(1)} %collective-permute-done.10.rest_4_) | copy-start | bytes 49156
  176.1 45.4 %all-to-all-start.1 = ((f32[32,1,64]{2,1,0:T(1,128)}), f32[32,1,64]{2,1,0:T(1,128)S(1)}, u32[]{:S(2)}, u32[]{:S(2)}) async-start(f32[32,1,64]{2,1,0:T(1,128)} %broadcast_in_dim.12), calls=%async_computation.1 | async-start | bytes 32768 | tf_op jit(solution)/shard_map/all_to_all | solution.py:268
  187.9 32.2 %collective-permute-start.12 = (f32[32,128]{1,0:T(8,128)}, f32[32,128]{1,0:T(8,128)S(1)}, u32[]{:S(2)}, u32[]{:S(2)}) collective-permute-start(f32[32,128]{1,0:T(8,128)} %get-tuple-element.58), channel_id=1, source_target_pairs={{0,128},{128,256},{256,384},{384,512},{512,640},{640,768},{768,896... | collective-permute-start | bytes 49160 | tf_op jit(solution)/shard_map/ppermute | solution.py:252
  189.8 47.2 %collective-permute-start.13 = (f32[32,128]{1,0:T(8,128)}, f32[32,128]{1,0:T(8,128)S(1)}, u32[]{:S(2)}, u32[]{:S(2)}) collective-permute-start(f32[32,128]{1,0:T(8,128)} %get-tuple-element.59), channel_id=1, source_target_pairs={{128,0},{256,128},{384,256},{512,384},{640,512},{768,640},{896,768... | collective-permute-start | bytes 49160 | tf_op jit(solution)/shard_map/ppermute | solution.py:253
  193.5 43.6 %collective-permute-start.14 = (f32[32,128]{1,0:T(8,128)}, f32[32,128]{1,0:T(8,128)S(1)}, u32[]{:S(2)}, u32[]{:S(2)}) collective-permute-start(f32[32,128]{1,0:T(8,128)} %get-tuple-element.60), channel_id=1, source_target_pairs={{0,8},{8,16},{16,24},{24,32},{32,40},{40,48},{48,56},{56,64},{64,7... | collective-permute-start | bytes 49160 | tf_op jit(solution)/shard_map/ppermute | solution.py:252
  196.9 40.2 %collective-permute-start.15 = (f32[32,128]{1,0:T(8,128)}, f32[32,128]{1,0:T(8,128)S(1)}, u32[]{:S(2)}, u32[]{:S(2)}) collective-permute-start(f32[32,128]{1,0:T(8,128)} %get-tuple-element.61), channel_id=1, source_target_pairs={{8,0},{16,8},{24,16},{32,24},{40,32},{48,40},{56,48},{64,56},{72,6... | collective-permute-start | bytes 49160 | tf_op jit(solution)/shard_map/ppermute | solution.py:253
  199.4 37.8 %collective-permute-start.16 = (f32[32,128]{1,0:T(8,128)}, f32[32,128]{1,0:T(8,128)S(1)}, u32[]{:S(2)}, u32[]{:S(2)}) collective-permute-start(f32[32,128]{1,0:T(8,128)} %get-tuple-element.62), channel_id=1, source_target_pairs={{0,1},{1,2},{2,3},{3,4},{4,5},{5,6},{6,7},{8,9},{9,10},{10,11},{11... | collective-permute-start | bytes 49160 | tf_op jit(solution)/shard_map/ppermute | solution.py:252
  220.2 25.4 %copy-start.7 = (f32[32,128]{1,0:T(8,128)}, f32[32,128]{1,0:T(8,128)S(1)}, u32[]{:S(2)}) copy-start(f32[32,128]{1,0:T(8,128)S(1)} %collective-permute-done.12.rest_0_) | copy-start | bytes 49156
  220.2 25.4 %collective-permute-start.17 = (f32[32,128]{1,0:T(8,128)}, f32[32,128]{1,0:T(8,128)S(1)}, u32[]{:S(2)}, u32[]{:S(2)}) collective-permute-start(f32[32,128]{1,0:T(8,128)} %get-tuple-element.63), channel_id=1, source_target_pairs={{1,0},{2,1},{3,2},{4,3},{5,4},{6,5},{7,6},{9,8},{10,9},{11,10},{12... | collective-permute-start | bytes 49160 | tf_op jit(solution)/shard_map/ppermute | solution.py:253
  237.1 8.5 %copy-start.8 = (f32[32,128]{1,0:T(8,128)}, f32[32,128]{1,0:T(8,128)S(1)}, u32[]{:S(2)}) copy-start(f32[32,128]{1,0:T(8,128)S(1)} %collective-permute-done.13.rest_1_) | copy-start | bytes 49156
  237.1 8.5 %copy-start.9 = (f32[32,128]{1,0:T(8,128)}, f32[32,128]{1,0:T(8,128)S(1)}, u32[]{:S(2)}) copy-start(f32[32,128]{1,0:T(8,128)S(1)} %collective-permute-done.14.rest_2_) | copy-start | bytes 49156
  237.1 8.5 %copy-start.11 = (f32[32,128]{1,0:T(8,128)}, f32[32,128]{1,0:T(8,128)S(1)}, u32[]{:S(2)}) copy-start(f32[32,128]{1,0:T(8,128)S(1)} %collective-permute-done.15.rest_3_) | copy-start | bytes 49156
  237.1 8.5 %copy-start.13 = (f32[32,128]{1,0:T(8,128)}, f32[32,128]{1,0:T(8,128)S(1)}, u32[]{:S(2)}) copy-start(f32[32,128]{1,0:T(8,128)S(1)} %collective-permute-done.16.rest_4_) | copy-start | bytes 49156
  (8 other events, 11.6 us)
where the time goes:
time: 252 us; the launch traced here: 251 us
  starting transfers between devices  111 us (44%)
  Pallas kernels  64.1 us (25%)
  waiting for transfers between devices  41.7 us (17%)
  blocking collectives  27.3 us (11%)
  local copies, waits for them, and re-layouts  5.12 us (2%)
    ppermute x9, starting transfers between devices, exchange(): before = lax.ppermute(high, axis, up)  77.2 us
    pallas_call x7, Pallas kernels, call(): pl.pallas_call(kernel, out_shape=outs, in_specs=in_specs, out_specs=[VMEM...  64.1 us
    ppermute x9, waiting for transfers between devices, exchange(): after = lax.ppermute(low, axis, down)  41.6 us
    all_to_all x2, blocking collectives, swap(): return lax.all_to_all(x, axes, 0, 0, axis_index_groups=groups, tiled=True)  27.3 us
    ppermute x9, starting transfers between devices, exchange(): after = lax.ppermute(low, axis, down)  22.1 us
    all_to_all x1, starting transfers between devices, swap(): return lax.all_to_all(x, axes, 0, 0, axis_index_groups=groups, tiled=True)  11.8 us
  transfers between devices with their start and end apart: 19, of which 4 were waited for; matrix products, arithmetic and copies ran while one was open for 1% of the time, Pallas kernels for 15%

commit v1 on v0

--- a/solution.py
+++ b/solution.py
@@ -36,14 +36,10 @@
     return jnp.broadcast_to(row, (8, B))
 
 
-def pivot_group(rows, g, lane, sub):
-    base = 8 * g
-    inside = (lane >= base) & (lane < base + 8)
+def clear_pivots(row, own, base, sub):
     mine = [
-        jnp.take_along_axis(rows[g], jnp.full((8, B), base + j, jnp.int32), axis=1)
-        for j in range(8)
+        jnp.take_along_axis(row, jnp.full((8, B), base + j, jnp.int32), axis=1) for j in range(8)
     ]
-    own = jnp.where(inside, jnp.where(lane - base == sub, 1.0, 0.0), rows[g])
     for p in range(0, 8, 2):
         c0, c1 = mine[p], mine[p + 1]
         a, b, c = spread(c0[p : p + 1]), spread(c1[p : p + 1]), spread(c1[p + 1 : p + 2])
@@ -59,26 +55,42 @@
         for j in range(p + 2, 8):
             mine[j] = clear(mine[j])
         own = clear(own)
-    parts = [spread(own[j : j + 1]) for j in range(8)]
-    new = []
-    for v, old in enumerate(rows):
-        out = own
-        if v != g:
-            out = jnp.where(inside, 0.0, old)
-            for j in range(8):
-                out = out - spread(old[:, base + j : base + j + 1]) * parts[j]
-        new.append(out)
-    return new
+    return own
+
+
+def clear_rows(rows, which, own, base, inside=None):
+    old = {v: rows[v] for v in which}
+    if inside is not None:
+        for v in which:
+            rows[v] = jnp.where(inside, 0.0, rows[v])
+    for j in range(8):
+        part = spread(own[j : j + 1])
+        for v in which:
+            rows[v] = rows[v] - spread(old[v][:, base + j : base + j + 1]) * part
+
+
+def sweep(rows, groups, start, lane, sub, exchange_pivots):
+    for g in range(groups):
+        base = start + 8 * g
+        own, inside = rows[g], None
+        if exchange_pivots:
+            inside = (lane >= base) & (lane < base + 8)
+            own = jnp.where(inside, jnp.where(lane - base == sub, 1.0, 0.0), own)
+        rows[g] = clear_pivots(rows[g], own, base, sub)
+        others = [v for v in range(len(rows)) if v != g]
+        clear_rows(rows, others, rows[g], base, inside)
+    return rows
+
+
+def iotas():
+    return (lax.broadcasted_iota(jnp.int32, (8, B), axis) for axis in (1, 0))
 
 
 def inverse(rows):
-    lane = lax.broadcasted_iota(jnp.int32, (8, B), 1)
-    sub = lax.broadcasted_iota(jnp.int32, (8, B), 0)
+    lane, sub = iotas()
 
     def body(_, carry):
-        rows = list(carry)
-        for g in range(GROUPS):
-            rows = pivot_group(rows, g, lane, sub)
+        rows = sweep(list(carry), GROUPS, 0, lane, sub, True)
         rows = rows[GROUPS:] + rows[:GROUPS]
         return tuple(pltpu.roll(row, B - 8 * GROUPS, 1) for row in rows)
 
@@ -201,26 +213,19 @@
         parts[2 * R :, at] = (left - middle.astype(F32)).astype(jnp.bfloat16)
     full = jnp.dot(parts[...], schur_ref[...], preferred_element_type=F32)
     image[...] = full[2 * R :] + full[R : 2 * R] + full[:R]
-    gram[:R, :] = rho
-    gram[R:, :] = mmt(zeta[...], image[...])
+    gram[:, :R] = rho
+    gram[:, R:] = mmt(zeta[...], image[...])
     for face in range(6):
         sends[face][...] = image[:, block(map_ref[face])]
 
 
 def finish_kernel(map_ref, gram_ref, zeta_ref, image_ref, residual_ref, *rest):
-    received, (solution_ref, out_ref, image) = rest[:6], rest[6:]
-    sub = lax.broadcasted_iota(jnp.int32, (8, 2 * R), 0)
-    joined = jnp.concatenate([gram_ref[:R, :], gram_ref[R:, :]], axis=1)
+    received, (solution_ref, out_ref, image, joined) = rest[:6], rest[6:]
+    lane, sub = iotas()
+    joined[...] = jnp.zeros((R, B), F32)
+    joined[:, : 2 * R] = gram_ref[...]
     rows = [joined[8 * v : 8 * v + 8, :] for v in range(R // 8)]
-    for p in range(R):
-        group, s = divmod(p, 8)
-        pivot = rows[group][s : s + 1, :]
-        pivot = pivot / pivot[:, R + p : R + p + 1]
-        new = []
-        for v, old in enumerate(rows):
-            out = old - old[:, R + p : R + p + 1] * pivot
-            new.append(jnp.where(sub == s, pivot, out) if v == group else out)
-        rows = new
+    rows = sweep(rows, R // 8, R, lane, sub, False)
     alpha = jnp.concatenate(rows, axis=0)[:, :R]
     image[...] = image_ref[...]
     for face in range(6):
@@ -303,7 +308,7 @@
     zeta_met = (*exchange("gx", *faces[:2]), *exchange("gy", *faces[2:]), *z_met)
     zeta, image, residual, gram, *faces = call(
         apply_kernel,
-        [arr(R, M)] * 3 + [arr(2 * R, R)] + [arr(R, B)] * 6,
+        [arr(R, M)] * 3 + [arr(R, 2 * R)] + [arr(R, B)] * 6,
         (place, stored, right_side, zeta_local, *zeta_met, *met),
         [pltpu.VMEM((3 * R, M), jnp.bfloat16)],
         10**9,
@@ -314,7 +319,7 @@
         finish_kernel,
         [arr(R, M)] * 2,
         (place, gram, zeta, image, residual, *image_met),
-        [pltpu.VMEM((R, M), F32)],
+        [pltpu.VMEM((R, M), F32), pltpu.VMEM((R, B), F32)],
         10**9,
     )
     return (solution[None, None, None], residual[None, None, None])

time: 252 us -> 247 us (0.980)
  starting transfers between devices: 111 us -> 128 us
  waiting for transfers between devices: 41.7 us -> 28.8 us
  Pallas kernels: 64.1 us -> 59.8 us
  blocking collectives: 27.3 us -> 24.2 us
    ppermute x9, waiting for transfers between devices: 41.6 us -> 27.5 us  [exchange(): after = lax.ppermute(low, axis, down)]
    ppermute x9, starting transfers between devices: 77.2 us -> 86.4 us  [exchange(): before = lax.ppermute(high, axis, up)]
    all_to_all x1 -> x2, starting transfers between devices: 11.8 us -> 18.6 us  [swap(): return lax.all_to_all(x, axes, 0, 0, axis_index_groups=groups, tiled=True)]
    pallas_call x7, Pallas kernels: 64.1 us -> 59.8 us  [call(): pl.pallas_call(kernel, out_shape=outs, in_specs=in_specs, out_specs=[VMEM...]
    all_to_all x2 -> x1, blocking collectives: 27.3 us -> 24.2 us  [swap(): return lax.all_to_all(x, axes, 0, 0, axis_index_groups=groups, tiled=True)]
  transfers between devices with their start and end apart: 19 -> 20, of which waited for: 4 -> 3; matrix products, arithmetic and copies ran while one was open for 1% -> 0% of each run, Pallas kernels for 15% -> 15%
where the time goes in v1:
time: 247 us; the launch traced here: 246 us
  starting transfers between devices  128 us (52%)
  Pallas kernels  59.8 us (24%)
  waiting for transfers between devices  28.8 us (12%)
  blocking collectives  24.2 us (10%)
  local copies, waits for them, and re-layouts  3.69 us (1%)
    ppermute x9, starting transfers between devices, exchange(): before = lax.ppermute(high, axis, up)  86.4 us
    pallas_call x7, Pallas kernels, call(): pl.pallas_call(kernel, out_shape=outs, in_specs=in_specs, out_specs=[VMEM...  59.8 us
    ppermute x9, waiting for transfers between devices, exchange(): after = lax.ppermute(low, axis, down)  27.5 us
    all_to_all x1, blocking collectives, swap(): return lax.all_to_all(x, axes, 0, 0, axis_index_groups=groups, tiled=True)  24.2 us
    ppermute x9, starting transfers between devices, exchange(): after = lax.ppermute(low, axis, down)  23.4 us
    all_to_all x2, starting transfers between devices, swap(): return lax.all_to_all(x, axes, 0, 0, axis_index_groups=groups, tiled=True)  18.6 us
  transfers between devices with their start and end apart: 20, of which 3 were waited for; matrix products, arithmetic and copies ran while one was open for 0% of the time, Pallas kernels for 15%

profile of v1, /device:TPU:34, one launch (start us, length us, event | category | flops | bytes accessed | tf_op | source)
XLA Modules:
  0.0 246.1 jit_solution(5100871806530407799)
XLA Ops:
  0.6 2.4 shard_map.51
  3.1 1.9 collective-permute-start
  5.0 3.6 %collective-permute-start.1 = (f32[160,128]{1,0:T(8,128)}, f32[160,128]{1,0:T(8,128)S(1)}, u32[]{:S(2)}, u32[]{:S(2)}) collective-permute-start(f32[160,128]{1,0:T(8,128)} %get-tuple-element.39), channel_id=1, source_target_pairs={{128,0},{256,128},{384,256},{512,384},{640,512},{768,640},{896,768... | collective-permute-start | bytes 245768 | tf_op jit(solution)/shard_map/ppermute | solution.py:258
  8.6 3.8 %collective-permute-start.2 = (f32[160,128]{1,0:T(8,128)}, f32[160,128]{1,0:T(8,128)S(1)}, u32[]{:S(2)}, u32[]{:S(2)}) collective-permute-start(f32[160,128]{1,0:T(8,128)} %get-tuple-element.40), channel_id=1, source_target_pairs={{0,8},{8,16},{16,24},{24,32},{32,40},{40,48},{48,56},{56,64},{64,7... | collective-permute-start | bytes 245768 | tf_op jit(solution)/shard_map/ppermute | solution.py:257
  12.5 2.0 collective-permute-start.3
  14.5 28.2 %collective-permute-start.4 = (f32[160,128]{1,0:T(8,128)}, f32[160,128]{1,0:T(8,128)S(1)}, u32[]{:S(2)}, u32[]{:S(2)}) collective-permute-start(f32[160,128]{1,0:T(8,128)} %get-tuple-element.45), channel_id=1, source_target_pairs={{0,1},{1,2},{2,3},{3,4},{4,5},{5,6},{6,7},{8,9},{9,10},{10,11},{11... | collective-permute-start | bytes 245768 | tf_op jit(solution)/shard_map/ppermute | solution.py:257
  42.7 14.4 %shard_map.50 = (f32[1056,256]{1,0:T(8,128)}, f32[800,256]{1,0:T(8,128)}, f32[544,256]{1,0:T(8,128)}, f32[288,256]{1,0:T(8,128)}) custom-call(s32[8]{0:T(128)} %bitcast.20, bf16[1024,1024]{1,0:T(8,128)(2,1)} %bitcast.11, f32[32,1024]{1,0:T(8,128)} %bitcast.14), custom_call_target="tpu_custom_call" | custom-call | flops 10000000000 | bytes 4980768 | tf_op jit(solution)/shard_map/pallas_call | solution.py:244
  57.1 1.5 collective-permute-start.5
  59.3 22.0 %shard_map.52 = (f32[800,256]{1,0:T(8,128)}, f32[544,256]{1,0:T(8,128)}, f32[288,256]{1,0:T(8,128)}) custom-call(f32[800,256]{1,0:T(8,128)} %get-tuple-element.35.i1, f32[544,256]{1,0:T(8,128)} %get-tuple-element.36.i2, f32[288,256]{1,0:T(8,128)} %get-tuple-element.37.i3, f32[160,128]{1,0:T(8,128)} %copy-done.1, f32[160,128]{1,0:T(8,128)} %copy-done.2, ...), custom_call_target="tpu_custom_call" | custom-call | flops 20000000000 | bytes 3670016 | tf_op jit(solution)/shard_map/pallas_call | solution.py:244
  81.3 11.8 %collective-permute-done.5.z1.rest_11_ = f32[160,128]{1,0:T(8,128)S(1)} collective-permute-done((f32[160,128]{1,0:T(8,128)S(1)}, f32[160,128]{1,0:T(8,128)S(1)}, u32[]{:S(2)}, u32[]{:S(2)}) %collective-permute-start.5) | collective-permute-done | bytes 81952 | tf_op jit(solution)/shard_map/ppermute | solution.py:258
  93.1 0.6 copy-done.6
  93.7 10.2 %shard_map.53 = (f32[32,128]{1,0:T(8,128)}, f32[32,128]{1,0:T(8,128)}) custom-call(f32[288,256]{1,0:T(8,128)} %get-tuple-element.44.i3, f32[160,128]{1,0:T(8,128)} %copy-done.5, f32[160,128]{1,0:T(8,128)} %copy-done.6), custom_call_target="tpu_custom_call" | custom-call | flops 10000000000 | bytes 491520 | tf_op jit(solution)/shard_map/pallas_call | solution.py:244
  103.9 4.4 %shard_map.54 = (f32[32,1024]{1,0:T(8,128)}, f32[32,128]{1,0:T(8,128)}, f32[32,128]{1,0:T(8,128)}, f32[32,128]{1,0:T(8,128)}, f32[32,128]{1,0:T(8,128)}) custom-call(f32[1056,256]{1,0:T(8,128)} %get-tuple-element.34.c0, f32[800,256]{1,0:T(8,128)} %get-tuple-element.42.c1, f32[544,256]{1,0:T(8,128)} %get-tuple-element.43.c2, f32[32,128]{1,0:T(8,128)} %get-tuple-element.47.z0, ...), custom_call_target="tpu_custom_call" | custom-call | flops 1000000000 | bytes 2686976 | tf_op jit(solution)/shard_map/pallas_call | solution.py:244
  108.3 1.9 collective-permute-start.6
  110.2 1.3 collective-permute-start.11
  111.5 3.6 %collective-permute-start.7 = (f32[32,128]{1,0:T(8,128)}, f32[32,128]{1,0:T(8,128)S(1)}, u32[]{:S(2)}, u32[]{:S(2)}) collective-permute-start(f32[32,128]{1,0:T(8,128)} %get-tuple-element.51), channel_id=1, source_target_pairs={{128,0},{256,128},{384,256},{512,384},{640,512},{768,640},{896,768... | collective-permute-start | bytes 49160 | tf_op jit(solution)/shard_map/ppermute | solution.py:258
  115.2 1.9 collective-permute-start.8
  117.1 3.9 %collective-permute-start.9 = (f32[32,128]{1,0:T(8,128)}, f32[32,128]{1,0:T(8,128)S(1)}, u32[]{:S(2)}, u32[]{:S(2)}) collective-permute-start(f32[32,128]{1,0:T(8,128)} %get-tuple-element.53), channel_id=1, source_target_pairs={{8,0},{16,8},{24,16},{32,24},{40,32},{48,40},{56,48},{64,56},{72,6... | collective-permute-start | bytes 49160 | tf_op jit(solution)/shard_map/ppermute | solution.py:258
  121.1 22.6 %collective-permute-start.10 = (f32[32,128]{1,0:T(8,128)S(1)}, f32[32,128]{1,0:T(8,128)S(1)}, u32[]{:S(2)}, u32[]{:S(2)}) collective-permute-start(f32[32,128]{1,0:T(8,128)S(1)} %copy-done.15), channel_id=1, source_target_pairs={{0,1},{1,2},{2,3},{3,4},{4,5},{5,6},{6,7},{8,9},{9,10},{10,11},{11... | collective-permute-start | bytes 49160 | tf_op jit(solution)/shard_map/ppermute | solution.py:257
  143.7 1.3 collective-permute-done.10.rest_4_
  145.7 3.5 %shard_map.55 = (f32[32,1024]{1,0:T(8,128)}, f32[32,1024]{1,0:T(8,128)}, f32[32,1024]{1,0:T(8,128)}, f32[32,64]{1,0:T(8,128)}, f32[32,128]{1,0:T(8,128)}, /*inde...) custom-call(s32[8]{0:T(128)} %bitcast.21, ...), custom_call_target="tpu_custom_call" | custom-call | flops 1000000000 | bytes 3448864 | tf_op jit(solution)/shard_map/pallas_call | solution.py:244
  149.2 24.2 %all_to_all.23 = f32[32,1,64]{2,1,0:T(1,128)S(1)} all-to-all(f32[32,1,64]{2,1,0:T(1,128)} %bitcast.18), channel_id=1, replica_groups={{0,2,4,6,128,130,132,134,256,258,260,262,384,386,388,390,512,514,516,51..., dimensions={0} | all-to-all | bytes 16384 | tf_op jit(solution)/shard_map/all_to_all | solution.py:273
  174.1 10.9 %all-to-all-start.1 = ((f32[32,1,64]{2,1,0:T(1,128)}), f32[32,1,64]{2,1,0:T(1,128)S(1)}, u32[]{:S(2)}, u32[]{:S(2)}) async-start(f32[32,1,64]{2,1,0:T(1,128)} %broadcast_in_dim.12), calls=%async_computation.1 | async-start | bytes 32768 | tf_op jit(solution)/shard_map/all_to_all | solution.py:273
  185.0 1.9 collective-permute-start.12
  186.9 3.6 %collective-permute-start.13 = (f32[32,128]{1,0:T(8,128)}, f32[32,128]{1,0:T(8,128)S(1)}, u32[]{:S(2)}, u32[]{:S(2)}) collective-permute-start(f32[32,128]{1,0:T(8,128)} %get-tuple-element.59), channel_id=1, source_target_pairs={{128,0},{256,128},{384,256},{512,384},{640,512},{768,640},{896,768... | collective-permute-start | bytes 49160 | tf_op jit(solution)/shard_map/ppermute | solution.py:258
  190.5 3.4 %collective-permute-start.14 = (f32[32,128]{1,0:T(8,128)}, f32[32,128]{1,0:T(8,128)S(1)}, u32[]{:S(2)}, u32[]{:S(2)}) collective-permute-start(f32[32,128]{1,0:T(8,128)} %get-tuple-element.60), channel_id=1, source_target_pairs={{0,8},{8,16},{16,24},{24,32},{32,40},{40,48},{48,56},{56,64},{64,7... | collective-permute-start | bytes 49160 | tf_op jit(solution)/shard_map/ppermute | solution.py:257
  193.9 2.5 %collective-permute-start.15 = (f32[32,128]{1,0:T(8,128)}, f32[32,128]{1,0:T(8,128)S(1)}, u32[]{:S(2)}, u32[]{:S(2)}) collective-permute-start(f32[32,128]{1,0:T(8,128)} %get-tuple-element.61), channel_id=1, source_target_pairs={{8,0},{16,8},{24,16},{32,24},{40,32},{48,40},{56,48},{64,56},{72,6... | collective-permute-start | bytes 49160 | tf_op jit(solution)/shard_map/ppermute | solution.py:258
  196.4 20.8 %collective-permute-start.16 = (f32[32,128]{1,0:T(8,128)}, f32[32,128]{1,0:T(8,128)S(1)}, u32[]{:S(2)}, u32[]{:S(2)}) collective-permute-start(f32[32,128]{1,0:T(8,128)} %get-tuple-element.62), channel_id=1, source_target_pairs={{0,1},{1,2},{2,3},{3,4},{4,5},{5,6},{6,7},{8,9},{9,10},{10,11},{11... | collective-permute-start | bytes 49160 | tf_op jit(solution)/shard_map/ppermute | solution.py:257
  217.2 1.3 collective-permute-start.17
  219.2 7.7 %all-to-all-start.2 = ((f32[32,1,64]{2,1,0:T(1,128)}), f32[32,1,64]{2,1,0:T(1,128)S(1)}, u32[]{:S(2)}, u32[]{:S(2)}) async-start(f32[32,1,64]{2,1,0:T(1,128)} %broadcast_in_dim.13), calls=%async_computation.2 | async-start | bytes 32768 | tf_op jit(solution)/shard_map/all_to_all | solution.py:273
  226.9 15.7 %collective-permute-done.17.rest_5_ = f32[32,128]{1,0:T(8,128)S(1)} collective-permute-done((f32[32,128]{1,0:T(8,128)}, f32[32,128]{1,0:T(8,128)S(1)}, u32[]{:S(2)}, u32[]{:S(2)}) %collective-permute-start.17) | collective-permute-done | bytes 16416 | tf_op jit(solution)/shard_map/ppermute | solution.py:258
  243.2 2.9 %shard_map.56 = (f32[32,1024]{1,0:T(8,128)}, f32[32,1024]{1,0:T(8,128)}) custom-call(s32[8]{0:T(128)} %bitcast.22, f32[32,64]{1,0:T(8,128)} %bitcast.17, f32[32,1024]{1,0:T(8,128)} %get-tuple-element.55.zeta_ref, f32[32,1024]{1,0:T(8,128)} %get-tuple-element.56.image_ref, f32[32,1024]{1,0:T(8,128)} %get-tuple-element.57.residual_ref, f32[32,128]{1,0:T(8,128)} %copy-done.8, ...), custom_call_target="tpu_custom_call" | custom-call | flops 1000000000 | bytes 761888 | tf_op jit(solution)/shard_map/pallas_call | solution.py:244
  (64 shorter events, 3.2 us)
Async XLA Ops:
  3.1 54.1 %collective-permute-start = (f32[160,128]{1,0:T(8,128)}, f32[160,128]{1,0:T(8,128)S(1)}, u32[]{:S(2)}, u32[]{:S(2)}) collective-permute-start(f32[160,128]{1,0:T(8,128)} %get-tuple-element.38), channel_id=1, source_target_pairs={{0,128},{128,256},{256,384},{384,512},{512,640},{640,768},{768,896... | collective-permute-start | bytes 245768 | tf_op jit(solution)/shard_map/ppermute | solution.py:257
  5.0 53.6 %collective-permute-start.1 = (f32[160,128]{1,0:T(8,128)}, f32[160,128]{1,0:T(8,128)S(1)}, u32[]{:S(2)}, u32[]{:S(2)}) collective-permute-start(f32[160,128]{1,0:T(8,128)} %get-tuple-element.39), channel_id=1, source_target_pairs={{128,0},{256,128},{384,256},{512,384},{640,512},{768,640},{896,768... | collective-permute-start | bytes 245768 | tf_op jit(solution)/shard_map/ppermute | solution.py:258
  8.6 50.0 %collective-permute-start.2 = (f32[160,128]{1,0:T(8,128)}, f32[160,128]{1,0:T(8,128)S(1)}, u32[]{:S(2)}, u32[]{:S(2)}) collective-permute-start(f32[160,128]{1,0:T(8,128)} %get-tuple-element.40), channel_id=1, source_target_pairs={{0,8},{8,16},{16,24},{24,32},{32,40},{40,48},{48,56},{56,64},{64,7... | collective-permute-start | bytes 245768 | tf_op jit(solution)/shard_map/ppermute | solution.py:257
  12.5 46.2 %collective-permute-start.3 = (f32[160,128]{1,0:T(8,128)}, f32[160,128]{1,0:T(8,128)S(1)}, u32[]{:S(2)}, u32[]{:S(2)}) collective-permute-start(f32[160,128]{1,0:T(8,128)} %get-tuple-element.41), channel_id=1, source_target_pairs={{8,0},{16,8},{24,16},{32,24},{40,32},{48,40},{56,48},{64,56},{72,6... | collective-permute-start | bytes 245768 | tf_op jit(solution)/shard_map/ppermute | solution.py:258
  14.5 42.6 %copy-start.7 = (f32[160,128]{1,0:T(8,128)S(1)}, f32[160,128]{1,0:T(8,128)}, u32[]{:S(2)}) copy-start(f32[160,128]{1,0:T(8,128)} %get-tuple-element.46) | copy-start | bytes 245764
  14.5 66.8 %collective-permute-start.4 = (f32[160,128]{1,0:T(8,128)}, f32[160,128]{1,0:T(8,128)S(1)}, u32[]{:S(2)}, u32[]{:S(2)}) collective-permute-start(f32[160,128]{1,0:T(8,128)} %get-tuple-element.45), channel_id=1, source_target_pairs={{0,1},{1,2},{2,3},{3,4},{4,5},{5,6},{6,7},{8,9},{9,10},{10,11},{11... | collective-permute-start | bytes 245768 | tf_op jit(solution)/shard_map/ppermute | solution.py:257
  57.1 1.6 copy-start.1
  57.1 35.9 %collective-permute-start.5 = (f32[160,128]{1,0:T(8,128)S(1)}, f32[160,128]{1,0:T(8,128)S(1)}, u32[]{:S(2)}, u32[]{:S(2)}) collective-permute-start(f32[160,128]{1,0:T(8,128)S(1)} %copy-done.7), channel_id=1, source_target_pairs={{1,0},{2,1},{3,2},{4,3},{5,4},{6,5},{7,6},{9,8},{10,9},{11,10},{12... | collective-permute-start | bytes 245768 | tf_op jit(solution)/shard_map/ppermute | solution.py:258
  81.3 11.8 %copy-start.5 = (f32[160,128]{1,0:T(8,128)}, f32[160,128]{1,0:T(8,128)S(1)}, u32[]{:S(2)}) copy-start(f32[160,128]{1,0:T(8,128)S(1)} %collective-permute-done.4.z0.rest_10_) | copy-start | bytes 245764
  103.9 6.3 %copy-start.17 = (f32[32,128]{1,0:T(8,128)S(1)}, f32[32,128]{1,0:T(8,128)}, u32[]{:S(2)}) copy-start(f32[32,128]{1,0:T(8,128)} %get-tuple-element.47.z0) | copy-start | bytes 49156
  103.9 17.1 %copy-start.15 = (f32[32,128]{1,0:T(8,128)S(1)}, f32[32,128]{1,0:T(8,128)}, u32[]{:S(2)}) copy-start(f32[32,128]{1,0:T(8,128)} %get-tuple-element.48.z1) | copy-start | bytes 49156
  108.3 12.7 %collective-permute-start.6 = (f32[32,128]{1,0:T(8,128)}, f32[32,128]{1,0:T(8,128)S(1)}, u32[]{:S(2)}, u32[]{:S(2)}) collective-permute-start(f32[32,128]{1,0:T(8,128)} %get-tuple-element.50), channel_id=1, source_target_pairs={{0,128},{128,256},{256,384},{384,512},{512,640},{640,768},{768,896... | collective-permute-start | bytes 49160 | tf_op jit(solution)/shard_map/ppermute | solution.py:257
  110.2 33.5 %collective-permute-start.11 = (f32[32,128]{1,0:T(8,128)S(1)}, f32[32,128]{1,0:T(8,128)S(1)}, u32[]{:S(2)}, u32[]{:S(2)}) collective-permute-start(f32[32,128]{1,0:T(8,128)S(1)} %copy-done.17), channel_id=1, source_target_pairs={{1,0},{2,1},{3,2},{4,3},{5,4},{6,5},{7,6},{9,8},{10,9},{11,10},{12... | collective-permute-start | bytes 49160 | tf_op jit(solution)/shard_map/ppermute | solution.py:258
  111.5 32.1 %collective-permute-start.7 = (f32[32,128]{1,0:T(8,128)}, f32[32,128]{1,0:T(8,128)S(1)}, u32[]{:S(2)}, u32[]{:S(2)}) collective-permute-start(f32[32,128]{1,0:T(8,128)} %get-tuple-element.51), channel_id=1, source_target_pairs={{128,0},{256,128},{384,256},{512,384},{640,512},{768,640},{896,768... | collective-permute-start | bytes 49160 | tf_op jit(solution)/shard_map/ppermute | solution.py:258
  115.2 28.5 %collective-permute-start.8 = (f32[32,128]{1,0:T(8,128)}, f32[32,128]{1,0:T(8,128)S(1)}, u32[]{:S(2)}, u32[]{:S(2)}) collective-permute-start(f32[32,128]{1,0:T(8,128)} %get-tuple-element.52), channel_id=1, source_target_pairs={{0,8},{8,16},{16,24},{24,32},{32,40},{40,48},{48,56},{56,64},{64,7... | collective-permute-start | bytes 49160 | tf_op jit(solution)/shard_map/ppermute | solution.py:257
  117.1 26.6 %collective-permute-start.9 = (f32[32,128]{1,0:T(8,128)}, f32[32,128]{1,0:T(8,128)S(1)}, u32[]{:S(2)}, u32[]{:S(2)}) collective-permute-start(f32[32,128]{1,0:T(8,128)} %get-tuple-element.53), channel_id=1, source_target_pairs={{8,0},{16,8},{24,16},{32,24},{40,32},{48,40},{56,48},{64,56},{72,6... | collective-permute-start | bytes 49160 | tf_op jit(solution)/shard_map/ppermute | solution.py:258
  121.1 24.0 %copy-start.11 = (f32[32,128]{1,0:T(8,128)}, f32[32,128]{1,0:T(8,128)S(1)}, u32[]{:S(2)}) copy-start(f32[32,128]{1,0:T(8,128)S(1)} %collective-permute-done.6.rest_0_) | copy-start | bytes 49156
  121.1 24.0 %collective-permute-start.10 = (f32[32,128]{1,0:T(8,128)S(1)}, f32[32,128]{1,0:T(8,128)S(1)}, u32[]{:S(2)}, u32[]{:S(2)}) collective-permute-start(f32[32,128]{1,0:T(8,128)S(1)} %copy-done.15), channel_id=1, source_target_pairs={{0,1},{1,2},{2,3},{3,4},{4,5},{5,6},{6,7},{8,9},{9,10},{10,11},{11... | collective-permute-start | bytes 49160 | tf_op jit(solution)/shard_map/ppermute | solution.py:257
  143.7 1.4 copy-start.16
  174.1 44.5 %all-to-all-start.1 = ((f32[32,1,64]{2,1,0:T(1,128)}), f32[32,1,64]{2,1,0:T(1,128)S(1)}, u32[]{:S(2)}, u32[]{:S(2)}) async-start(f32[32,1,64]{2,1,0:T(1,128)} %broadcast_in_dim.12), calls=%async_computation.1 | async-start | bytes 32768 | tf_op jit(solution)/shard_map/all_to_all | solution.py:273
  185.0 32.2 %collective-permute-start.12 = (f32[32,128]{1,0:T(8,128)}, f32[32,128]{1,0:T(8,128)S(1)}, u32[]{:S(2)}, u32[]{:S(2)}) collective-permute-start(f32[32,128]{1,0:T(8,128)} %get-tuple-element.58), channel_id=1, source_target_pairs={{0,128},{128,256},{256,384},{384,512},{512,640},{640,768},{768,896... | collective-permute-start | bytes 49160 | tf_op jit(solution)/shard_map/ppermute | solution.py:257
  186.9 40.0 %collective-permute-start.13 = (f32[32,128]{1,0:T(8,128)}, f32[32,128]{1,0:T(8,128)S(1)}, u32[]{:S(2)}, u32[]{:S(2)}) collective-permute-start(f32[32,128]{1,0:T(8,128)} %get-tuple-element.59), channel_id=1, source_target_pairs={{128,0},{256,128},{384,256},{512,384},{640,512},{768,640},{896,768... | collective-permute-start | bytes 49160 | tf_op jit(solution)/shard_map/ppermute | solution.py:258
  190.5 36.4 %collective-permute-start.14 = (f32[32,128]{1,0:T(8,128)}, f32[32,128]{1,0:T(8,128)S(1)}, u32[]{:S(2)}, u32[]{:S(2)}) collective-permute-start(f32[32,128]{1,0:T(8,128)} %get-tuple-element.60), channel_id=1, source_target_pairs={{0,8},{8,16},{16,24},{24,32},{32,40},{40,48},{48,56},{56,64},{64,7... | collective-permute-start | bytes 49160 | tf_op jit(solution)/shard_map/ppermute | solution.py:257
  193.9 33.0 %collective-permute-start.15 = (f32[32,128]{1,0:T(8,128)}, f32[32,128]{1,0:T(8,128)S(1)}, u32[]{:S(2)}, u32[]{:S(2)}) collective-permute-start(f32[32,128]{1,0:T(8,128)} %get-tuple-element.61), channel_id=1, source_target_pairs={{8,0},{16,8},{24,16},{32,24},{40,32},{48,40},{56,48},{64,56},{72,6... | collective-permute-start | bytes 49160 | tf_op jit(solution)/shard_map/ppermute | solution.py:258
  196.4 30.5 %collective-permute-start.16 = (f32[32,128]{1,0:T(8,128)}, f32[32,128]{1,0:T(8,128)S(1)}, u32[]{:S(2)}, u32[]{:S(2)}) collective-permute-start(f32[32,128]{1,0:T(8,128)} %get-tuple-element.62), channel_id=1, source_target_pairs={{0,1},{1,2},{2,3},{3,4},{4,5},{5,6},{6,7},{8,9},{9,10},{10,11},{11... | collective-permute-start | bytes 49160 | tf_op jit(solution)/shard_map/ppermute | solution.py:257
  217.2 25.4 %copy-start.8 = (f32[32,128]{1,0:T(8,128)}, f32[32,128]{1,0:T(8,128)S(1)}, u32[]{:S(2)}) copy-start(f32[32,128]{1,0:T(8,128)S(1)} %collective-permute-done.12.rest_0_) | copy-start | bytes 49156
  217.2 25.4 %collective-permute-start.17 = (f32[32,128]{1,0:T(8,128)}, f32[32,128]{1,0:T(8,128)S(1)}, u32[]{:S(2)}, u32[]{:S(2)}) collective-permute-start(f32[32,128]{1,0:T(8,128)} %get-tuple-element.63), channel_id=1, source_target_pairs={{1,0},{2,1},{3,2},{4,3},{5,4},{6,5},{7,6},{9,8},{10,9},{11,10},{12... | collective-permute-start | bytes 49160 | tf_op jit(solution)/shard_map/ppermute | solution.py:258
  219.2 23.5 %all-to-all-start.2 = ((f32[32,1,64]{2,1,0:T(1,128)}), f32[32,1,64]{2,1,0:T(1,128)S(1)}, u32[]{:S(2)}, u32[]{:S(2)}) async-start(f32[32,1,64]{2,1,0:T(1,128)} %broadcast_in_dim.13), calls=%async_computation.2 | async-start | bytes 32768 | tf_op jit(solution)/shard_map/all_to_all | solution.py:273
  226.9 15.7 %copy-start.9 = (f32[32,128]{1,0:T(8,128)}, f32[32,128]{1,0:T(8,128)S(1)}, u32[]{:S(2)}) copy-start(f32[32,128]{1,0:T(8,128)S(1)} %collective-permute-done.13.rest_1_) | copy-start | bytes 49156
  226.9 15.7 %copy-start.10 = (f32[32,128]{1,0:T(8,128)}, f32[32,128]{1,0:T(8,128)S(1)}, u32[]{:S(2)}) copy-start(f32[32,128]{1,0:T(8,128)S(1)} %collective-permute-done.14.rest_2_) | copy-start | bytes 49156
  226.9 15.7 %copy-start.12 = (f32[32,128]{1,0:T(8,128)}, f32[32,128]{1,0:T(8,128)S(1)}, u32[]{:S(2)}) copy-start(f32[32,128]{1,0:T(8,128)S(1)} %collective-permute-done.15.rest_3_) | copy-start | bytes 49156
  226.9 15.7 %copy-start.14 = (f32[32,128]{1,0:T(8,128)}, f32[32,128]{1,0:T(8,128)S(1)}, u32[]{:S(2)}) copy-start(f32[32,128]{1,0:T(8,128)S(1)} %collective-permute-done.16.rest_4_) | copy-start | bytes 49156
  (10 other events, 8.5 us)
